TPU v7x, 256 devices: a whole 4x4x8 slice. The times are simulated.
256 devices in a mesh: gx: 4 (over y), gy: 8 (over x, core), gz: 8 (over z).
Axes of the slice: x: 4, y: 4, z: 8, core: 2. Of those that a mesh axis runs over, the one named last changes fastest.
Arguments:
- density: float32 [128, 256, 1024], P('gx', 'gy', 'gz'), may hold values from -3.5 to 3.5
- conductance: float32 [3, 128, 256, 1024], P(None, 'gx', 'gy', 'gz'), may hold values from 0.25 to 1
- decay_rate: float32 [128, 256, 1024], P('gx', 'gy', 'gz'), may hold values from 0.5 to 4
- diffusion_numbers: float32 [3], replicated, may hold values from 2 to 8
- plane_offset: int32 [1], replicated, may hold values from 0 to 1023
Outputs:
- updated: float32 [128, 256, 1024], P('gx', 'gy', 'gz')
All inputs are finite; a program needn't handle non-finite values.
Results may differ from a plain program's by a relative error of at most 0.0011.
Values sent between devices are 32-bit elements; how exact they have to be, the bound alone decides.
A program may use at most 64 MiB of HBM per device.

v0:
```python
import functools
import math

import jax
import jax.numpy as jnp
from jax import lax
from jax.experimental import pallas as pl
from jax.experimental.pallas import tpu as pltpu
from jax.sharding import PartitionSpec as P

MESH = pl.DeviceIdType.MESH
F32 = jnp.float32
AXES = ("gx", "gy", "gz")
WEIGHT = 0.5


def far_first(n):
    return sorted(range(1, n), key=lambda j: (-min(j, n - j), j))


def rows_loop(lo, count, step, body, carry, unroll):
    whole = count // unroll

    def block(k, c):
        for m in range(unroll):
            c = body(lo + step * (k * unroll + m), c)
        return c

    carry = lax.fori_loop(0, whole, block, carry)
    for m in range(whole * unroll, count):
        carry = body(lo + step * m, carry)
    return carry


def eliminate(excess, coupling, left, e):
    inverse = 1.0 / (excess + coupling + e)
    alpha, beta, leak = e * inverse, coupling * inverse, excess * inverse
    return inverse, alpha, beta, e * leak, e * beta, left + coupling * leak


def ring_factors(nodes):
    n = len(nodes)
    total = [nodes[j][1] + nodes[j - 1][2] for j in range(n)]
    alphas, betas = {}, {}
    coupling, excess, leak1 = nodes[1][0], total[2], total[1]
    for j in range(2, n):
        _, alphas[j], betas[j], carried, coupling, leak1 = eliminate(excess, coupling, leak1, nodes[j][0])
        excess = carried + total[(j + 1) % n]
    leak0 = excess
    c = nodes[0][0] + coupling
    inverse = 1.0 / (leak0 * leak1 + c * (leak0 + leak1))
    to0, to1 = {}, {}
    p, q = jnp.zeros_like(c), jnp.ones_like(c)
    for j in reversed(range(2, n)):
        p, q = betas[j] + alphas[j] * p, alphas[j] * q
        to1[j], to0[j] = p, q
    return [to0[j] for j in range(2, n)] + [to1[j] for j in range(2, n)] + [(leak1 + c) * inverse, c * inverse, (leak0 + c) * inverse]


def ring_apply(factors, loads):
    n = len(loads)
    right = [loads[j][0] + loads[j - 1][1] for j in range(n)]
    sum0, sum1 = right[0], right[1]
    for j in range(2, n):
        sum0 = sum0 + factors(j - 2) * right[j]
        sum1 = sum1 + factors(n - 2 + j - 2) * right[j]
    g00, g01, g11 = (factors(2 * (n - 2) + k) for k in range(3))
    return g00 * sum0 + g01 * sum1, g01 * sum0 + g11 * sum1


def kernel(
    sizes,
    diff_ref, offset_ref, v_hbm, c_hbm, dec_hbm, out_hbm,
    vx, cx, cy, cz, dec, vy, cyy, vz, czz,
    ax, bx, rx, ay, by, ry, az, bz, rz, segz,
    wx, wy, wz, work1, work2, work3,
    halo_x, halo_y, halo_z,
    mx_own, my_own, mz_own, mx_in, my_in, mz_in,
    fx_own, fy_own, fz_own, fx_in, fy_in, fz_in,
    load_sem, halo_send, halo_recv, mat_send, mat_recv, rhs_send, rhs_recv, out_sem,
):
    me = [lax.axis_index(a) for a in AXES]

    def peer(axis, shift):
        n = sizes[axis]
        return {AXES[axis]: lax.rem(me[axis] + (shift % n), n)}

    loads = [
        pltpu.make_async_copy(src, dst, load_sem.at[k])
        for k, (src, dst) in enumerate(((v_hbm, vx), (c_hbm.at[2], cz), (c_hbm.at[1], cy), (c_hbm.at[0], cx), (dec_hbm, dec)))
    ]
    for copy in loads:
        copy.start()

    barrier = pltpu.get_barrier_semaphore()
    for axis in range(3):
        for j in far_first(sizes[axis]):
            pl.semaphore_signal(barrier, inc=1, device_id=peer(axis, j), device_id_type=MESH)

    def remote(src, dst, send, recv, axis, shift):
        return pltpu.make_async_remote_copy(
            src_ref=src, dst_ref=dst, send_sem=send, recv_sem=recv, device_id=peer(axis, shift), device_id_type=MESH
        )

    scale = [diff_ref[a] * float(c * c) for a, c in enumerate((32, 32, 128))]
    half = [WEIGHT * s for s in scale]

    vx2, cy2, cz2, vz2, czz2 = (ref.reshape(1024, 128) for ref in (vx, cy, cz, vz, czz))

    loads[0].wait()
    loads[1].wait()

    def to_y(y, _):
        for xc in range(4):
            vy[xc, y] = vx2[pl.ds(xc * 256 + y, 8, stride=32), :]
            work1[xc, y] = cz2[pl.ds(xc * 256 + y, 8, stride=32), :]
        return 0

    rows_loop(0, 32, 1, to_y, 0, 4)

    def into_z(src, dst2):
        for b in range(8):
            block = src[b // 2, pl.ds(16 * (b % 2), 16)].reshape(128, 128)
            dst2[pl.ds(b, 128, stride=8), :] = block.T

    into_z(vy, vz2)
    into_z(work1, czz2)

    pl.semaphore_wait(barrier, sum(sizes) - 3)

    halos = [
        remote(vx.at[0], halo_x, halo_send.at[0], halo_recv.at[0], 0, -1),
        remote(v_hbm.at[:, 0, 0, :], halo_y.at[0], halo_send.at[1], halo_recv.at[1], 1, -1),
        remote(v_hbm.at[:, 3, 7, :], halo_y.at[1], halo_send.at[2], halo_recv.at[2], 1, 1),
        remote(c_hbm.at[1, :, 3, 7, :], halo_y.at[2], halo_send.at[3], halo_recv.at[3], 1, 1),
        remote(vz.at[0, 0], halo_z.at[0], halo_send.at[4], halo_recv.at[4], 2, -1),
        remote(vz.at[3, 31], halo_z.at[1], halo_send.at[5], halo_recv.at[5], 2, 1),
        remote(czz.at[3, 31], halo_z.at[2], halo_send.at[6], halo_recv.at[6], 2, 1),
    ]
    for copy in halos:
        copy.start()

    for copy in loads[2:]:
        copy.wait()

    def to_y2(y, _):
        for xc in range(4):
            cyy[xc, y] = cy2[pl.ds(xc * 256 + y, 8, stride=32), :]
        return 0

    rows_loop(0, 32, 1, to_y2, 0, 4)

    def excess_x(i):
        v = vx[i]
        return 1.0 + WEIGHT * (dec[i] * (1.0 + 3.0 * (v * v)))

    def matrix_row(i, carry):
        (kx, lx, sx), (ky, ly, sy), (kz, lz, sz) = carry
        rx[i], ax[i], bx[i], cx_l, kx, sx = eliminate(excess_x(i) + lx, kx, sx, half[0] * cx[i])
        ry[:, i], ay[:, i], by[:, i], cy_l, ky, sy = eliminate(1.0 + ly, ky, sy, half[1] * cyy[:, i])
        rz[:, i], az[:, i], bz[:, i], cz_l, kz, sz = eliminate(1.0 + lz, kz, sz, half[2] * czz[:, i])
        return (kx, cx_l, sx), (ky, cy_l, sy), (kz, cz_l, sz)

    zero = jnp.zeros((4, 8, 128), F32)
    start = (
        (half[0] * cx[0], zero, excess_x(0)),
        (half[1] * cyy[:, 0], zero, zero + 1.0),
        (half[2] * czz[:, 0], zero, zero + 1.0),
    )
    ends = rows_loop(1, 31, 1, matrix_row, start, 1)
    for own, (coupling, carried, left) in zip((mx_own, my_own), ends[:2]):
        own[0], own[1], own[2] = coupling, left, carried
    kz, lz, sz = ends[2]
    coupling, left, excess = kz[0], sz[0], sz[1] + lz[0]
    for s in range(1, 4):
        inverse, alpha, beta, carried, coupling, left = eliminate(excess, coupling, left, kz[s])
        segz[0, s], segz[1, s], segz[2, s] = inverse, alpha, beta
        excess = carried + lz[s] + (sz[s + 1] if s < 3 else 0.0)
    mz_own[0], mz_own[1], mz_own[2] = coupling, left, excess

    mats, first = [], 0
    for axis, own, into in ((0, mx_own, mx_in), (1, my_own, my_in), (2, mz_own, mz_in)):
        for j in far_first(sizes[axis]):
            k = first + j - 1
            mats.append(remote(own, into.at[j - 1], mat_send.at[k], mat_recv.at[k], axis, -j))
            mats[-1].start()
        first += sizes[axis] - 1
    mats_of = (mats[: sizes[0] - 1], mats[sizes[0] - 1 : sizes[0] + sizes[1] - 2], mats[sizes[0] + sizes[1] - 2 :])

    for copy in halos:
        copy.wait()

    hy = halo_y.reshape(3, 4, 8, 128)

    def flux_y(y, carry):
        v, below = carry
        after = vy[:, y + 1]
        flux = scale[1] * (cyy[:, y] * (after - v))
        work1[:, y] = flux - below
        return after, flux

    v0 = vy[:, 0]
    v_last, below = rows_loop(0, 31, 1, flux_y, (v0, scale[1] * (hy[2] * (v0 - hy[1]))), 4)
    work1[:, 31] = scale[1] * (cyy[:, 31] * (hy[0] - v_last)) - below

    def flux_z(i, carry):
        v, below = carry
        after = vz[:, i + 1]
        flux = scale[2] * (czz[:, i] * (after - v))
        work2[:, i] = flux - below
        return after, flux

    v0 = vz[:, 0]
    c31, v31 = czz[:, 31], vz[:, 31]
    prev_v = jnp.concatenate([halo_z[1][None], v31[:3]], axis=0)
    prev_c = jnp.concatenate([halo_z[2][None], c31[:3]], axis=0)
    next_v = jnp.concatenate([v0[1:], halo_z[0][None]], axis=0)
    v_last, below = rows_loop(0, 31, 1, flux_z, (v0, scale[2] * (prev_c * (v0 - prev_v))), 4)
    work2[:, 31] = scale[2] * (c31 * (next_v - v_last)) - below

    def from_z(src, dst, plus):
        src2 = src.reshape(1024, 128)
        for b in range(8):
            at = (b // 2, pl.ds(16 * (b % 2), 16))
            dst[at] = plus[at] + src2[pl.ds(b, 128, stride=8), :].T.reshape(16, 8, 128)

    from_z(work2, work1, work1)

    lane = lax.broadcasted_iota(jnp.int32, (1, 8, 128), 2)
    length = 128 * sizes[2]
    phase = lax.rem(lane + (me[2] * 128 + offset_ref[0]), length).astype(F32) * (2.0 * math.pi / length)
    forcing = 2.0 * jnp.sin(phase)

    work1_2 = work1.reshape(1024, 128)

    def right_x(i, v, after, below):
        flux = scale[0] * (cx[i] * (after - v))
        base = (i // 8) * 256 + i % 8
        rest = jnp.stack([work1_2[pl.ds(base + 64 * yc, 8, stride=8), :] for yc in range(4)])
        right = (flux - below) + rest - dec[i] * v * (1.0 + v * v) + forcing
        return right, flux

    def forward_x(i, carry):
        v, below, y, load = carry
        after = vx[i + 1]
        right, flux = right_x(i, v, after, below)
        y = right + ax[i - 1] * y
        work3[i] = y
        return after, flux, y, load + bx[i] * y

    v0, v1, v2 = vx[0], vx[1], vx[2]
    load, flux = right_x(0, v0, v1, zero)
    y, flux = right_x(1, v1, v2, flux)
    work3[1] = y
    v, below, y, load = rows_loop(2, 29, 1, forward_x, (v2, flux, y, load + bx[1] * y), 1)
    right, flux = right_x(31, v, halo_x[...], below)
    y = right + ax[30] * y
    work3[31] = y
    fx_own[0] = load + bx[31] * y
    fx_own[1] = ax[31] * y - flux

    def exchange(axis, own, into, first):
        copies = []
        for j in far_first(sizes[axis]):
            k = first + j - 1
            copies.append(remote(own, into.at[j - 1], rhs_send.at[k], rhs_recv.at[k], axis, -j))
            copies[-1].start()
        return copies

    def factors(axis, own, into, weights):
        for copy in mats_of[axis]:
            copy.wait_recv()
        nodes = [tuple(own[k] for k in range(3))] + [tuple(into[j, k] for k in range(3)) for j in range(sizes[axis] - 1)]
        for k, value in enumerate(ring_factors(nodes)):
            weights[k] = value

    def solve(axis, own, into, weights, copies):
        for copy in copies:
            copy.wait_recv()
        pairs = [(own[0], own[1])] + [(into[j, 0], into[j, 1]) for j in range(sizes[axis] - 1)]
        return ring_apply(lambda k: weights[k], pairs)

    sent_x = exchange(0, fx_own, fx_in, 0)
    factors(0, mx_own, mx_in, wx)
    factors(1, my_own, my_in, wy)
    factors(2, mz_own, mz_in, wz)
    node, after = solve(0, fx_own, fx_in, wx, sent_x)

    work1x = work1.reshape(32, 4, 8, 128)
    u = after

    def backward_x(i, u):
        u = (rx[i] * work3[i] + bx[i] * node) + ax[i] * u
        work1x[i] = u
        return u

    rows_loop(31, 31, -1, backward_x, u, 2)
    work1x[0] = node

    def right_y(y):
        return jnp.stack([work1_2[pl.ds(xc * 256 + y, 8, stride=32), :] for xc in range(4)])

    def forward_y(i, carry):
        y, load = carry
        y = right_y(i) + ay[:, i - 1] * y
        work2[:, i] = y
        return y, load + by[:, i] * y

    y = right_y(1)
    work2[:, 1] = y
    y, load = rows_loop(2, 30, 1, forward_y, (y, right_y(0) + by[:, 1] * y), 2)
    fy_own[0] = load
    fy_own[1] = ay[:, 31] * y

    sent_y = exchange(1, fy_own, fy_in, sizes[0] - 1)
    node_y, after_y = solve(1, fy_own, fy_in, wy, sent_y)

    def backward_y(i, u):
        u = (ry[:, i] * work2[:, i] + by[:, i] * node_y) + ay[:, i] * u
        work1[:, i] = u
        return u

    rows_loop(31, 31, -1, backward_y, after_y, 2)
    work1[:, 0] = node_y

    into_z(work1, work2.reshape(1024, 128))

    def forward_z(i, carry):
        y, load = carry
        y = work2[:, i] + az[:, i - 1] * y
        work3z[:, i] = y
        return y, load + bz[:, i] * y

    work3z = work3.reshape(4, 32, 8, 128)
    y = work2[:, 1]
    work3z[:, 1] = y
    y, load = rows_loop(2, 30, 1, forward_z, (y, work2[:, 0] + bz[:, 1] * y), 2)
    carried = az[:, 31] * y
    ys, left = [None], load[0]
    for s in range(1, 4):
        y = load[s] + carried[s - 1]
        if s > 1:
            y = y + segz[1, s - 1] * ys[-1]
        ys.append(y)
        left = left + segz[2, s] * y
    fz_own[0] = left
    fz_own[1] = carried[3] + segz[1, 3] * ys[3]

    sent_z = exchange(2, fz_own, fz_in, sizes[0] + sizes[1] - 2)
    node_z, after_z = solve(2, fz_own, fz_in, wz, sent_z)
    ends_z = [after_z]
    for s in (3, 2, 1):
        ends_z.insert(0, (segz[0, s] * ys[s] + segz[2, s] * node_z) + segz[1, s] * ends_z[0])
    starts_z = jnp.stack([node_z] + ends_z[:3])

    def backward_z(i, u):
        u = (rz[:, i] * work3z[:, i] + bz[:, i] * starts_z) + az[:, i] * u
        work2[:, i] = u
        return u

    rows_loop(31, 31, -1, backward_z, jnp.stack(ends_z), 2)
    work2[:, 0] = starts_z

    from_z(work2, work1, vy)

    def to_x(y, _):
        for xc in range(4):
            vx2[pl.ds(xc * 256 + y, 8, stride=32), :] = work1[xc, y]
        return 0

    for copy in mats + sent_x + sent_y + sent_z:
        copy.wait_send()
    rows_loop(0, 32, 1, to_x, 0, 4)
    out = pltpu.make_async_copy(vx, out_hbm, out_sem)
    out.start()
    out.wait()


def on_device(sizes, density, conductance, decay_rate, diffusion_numbers, plane_offset):
    nx, ny, nz = sizes
    grid = (32, 4, 8, 128)
    lines = (4, 32, 8, 128)
    one = (4, 8, 128)
    peers = nx + ny + nz - 3
    vmem = lambda *shape: pltpu.VMEM(shape, F32)
    dma = lambda n: pltpu.SemaphoreType.DMA((n,))
    anywhere = pl.BlockSpec(memory_space=pl.ANY)
    scalar = pl.BlockSpec(memory_space=pltpu.SMEM)
    updated = pl.pallas_call(
        functools.partial(kernel, sizes),
        out_shape=jax.ShapeDtypeStruct(grid, F32),
        in_specs=[scalar, scalar, anywhere, anywhere, anywhere],
        out_specs=anywhere,
        scratch_shapes=[vmem(*grid)] * 5
        + [vmem(*lines)] * 4
        + [vmem(*grid)] * 3
        + [vmem(*lines)] * 6
        + [vmem(3, 4, 8, 128)]
        + [vmem(2 * nx - 1, *one), vmem(2 * ny - 1, *one), vmem(2 * nz - 1, 8, 128)]
        + [vmem(*lines), vmem(*lines), vmem(*grid)]
        + [vmem(*one), vmem(3, 32, 128), vmem(3, 8, 128)]
        + [vmem(3, *one), vmem(3, *one), vmem(3, 8, 128)]
        + [vmem(nx - 1, 3, *one), vmem(ny - 1, 3, *one), vmem(nz - 1, 3, 8, 128)]
        + [vmem(2, *one), vmem(2, *one), vmem(2, 8, 128)]
        + [vmem(nx - 1, 2, *one), vmem(ny - 1, 2, *one), vmem(nz - 1, 2, 8, 128)]
        + [dma(5), dma(7), dma(7), dma(peers), dma(peers), dma(peers), dma(peers), pltpu.SemaphoreType.DMA],
        compiler_params=pltpu.CompilerParams(collective_id=0, has_side_effects=True, vmem_limit_bytes=48 * 1024 * 1024),
        name="adi_step",
    )(
        diffusion_numbers,
        plane_offset,
        density.reshape(grid),
        conductance.reshape((3,) + grid),
        decay_rate.reshape(grid),
    )
    return updated.reshape(density.shape)


def solution(mesh):
    sizes = tuple(mesh.shape[a] for a in AXES)
    placed = (P("gx", "gy", "gz"), P(None, "gx", "gy", "gz"), P("gx", "gy", "gz"), P(), P())
    return jax.shard_map(
        functools.partial(on_device, sizes), mesh=mesh, in_specs=placed, out_specs=P("gx", "gy", "gz"), check_vma=False
    )
```

profile of v0, /device:TPU:1, one launch (start us, length us, event | category | flops | bytes accessed | tf_op | source)
XLA Modules:
  0.0 36.5 jit_solution(16142942051380759599)
XLA Ops:
  0.7 0.0 copy-start
  0.7 1.4 %copy-done = f32[3,32,32,128]{3,2,1,0:T(8,128)S(1)} copy-done((f32[3,32,32,128]{3,2,1,0:T(8,128)S(1)}, f32[3,32,32,128]{3,2,1,0:T(8,128)}, u32[]{:S(2)}) %copy-start) | copy-done | bytes 1572888
  2.1 0.0 copy-start.1
  2.1 1.0 %copy-done.1 = f32[32,32,128]{2,1,0:T(8,128)S(1)} copy-done((f32[32,32,128]{2,1,0:T(8,128)S(1)}, f32[32,32,128]{2,1,0:T(8,128)}, u32[]{:S(2)}) %copy-start.1) | copy-done | bytes 524312
  3.1 0.0 copy-start.2
  3.1 1.0 %copy-done.2 = f32[32,32,128]{2,1,0:T(8,128)S(1)} copy-done((f32[32,32,128]{2,1,0:T(8,128)S(1)}, f32[32,32,128]{2,1,0:T(8,128)}, u32[]{:S(2)}) %copy-start.2) | copy-done | bytes 524312
  4.1 0.0 copy-start.3
  4.1 0.7 %copy-done.3 = f32[3]{0:T(128)S(1)} copy-done((f32[3]{0:T(128)S(1)}, f32[3]{0:T(128)}, u32[]{:S(2)}) %copy-start.3) | copy-done | bytes 36
  4.8 30.9 %adi_step.1 = f32[32,4,8,128]{3,2,1,0:T(8,128)S(1)} custom-call(f32[3]{0:T(128)S(1)} %copy-done.3, s32[1]{0:T(128)S(6)} %copy.7.offset_ref, f32[32,4,8,128]{3,2,1,0:T(8,128)S(1)} %bitcast.6, f32[3,32,4,8,128]{4,3,2,1,0:T(8,128)S(1)} %bitcast.5, f32[32,4,8,128]{3,2,1,0:T(8,128)S(1)} %bitcast.7), custom_call_target="tpu_custom_call" | custom-call | tf_op jit(solution)/shard_map/adi_step/pallas_call | solution.py:389
  35.7 0.8 %copy.8 = f32[32,32,128]{2,1,0:T(8,128)} copy(f32[32,32,128]{2,1,0:T(8,128)S(1)} %bitcast.4) | data formatting | bytes 1048576
Async XLA Ops:
  0.7 1.4 %copy-start = (f32[3,32,32,128]{3,2,1,0:T(8,128)S(1)}, f32[3,32,32,128]{3,2,1,0:T(8,128)}, u32[]{:S(2)}) copy-start(f32[3,32,32,128]{3,2,1,0:T(8,128)} %param.6) | copy-start | bytes 4718596
  2.1 1.0 %copy-start.1 = (f32[32,32,128]{2,1,0:T(8,128)S(1)}, f32[32,32,128]{2,1,0:T(8,128)}, u32[]{:S(2)}) copy-start(f32[32,32,128]{2,1,0:T(8,128)} %param.5) | copy-start | bytes 1572868
  3.1 1.0 %copy-start.2 = (f32[32,32,128]{2,1,0:T(8,128)S(1)}, f32[32,32,128]{2,1,0:T(8,128)}, u32[]{:S(2)}) copy-start(f32[32,32,128]{2,1,0:T(8,128)} %param.7) | copy-start | bytes 1572868
  4.1 0.7 %copy-start.3 = (f32[3]{0:T(128)S(1)}, f32[3]{0:T(128)}, u32[]{:S(2)}) copy-start(f32[3]{0:T(128)} %diff_ref.1) | copy-start | bytes 40
where the time goes:
time: 36.7 us; the launch traced here: 36.5 us
  Pallas kernels  30.9 us (84%)
  local copies, waits for them, and re-layouts  4.93 us (13%)
  between operations  0.67 us (2%)
    pallas_call x1, Pallas kernels, on_device(): pl.pallas_call(functools.partial(kernel, sizes), out_shape=jax.ShapeDtype...  30.9 us
    unnamed x9, local copies, waits for them, and re-layouts  4.93 us

commit v1 on v0

v1 whole, which is shorter than its diff:
```python
import functools
import math

import jax
import jax.numpy as jnp
from jax import lax
from jax.experimental import pallas as pl
from jax.experimental.pallas import tpu as pltpu
from jax.sharding import PartitionSpec as P

MESH = pl.DeviceIdType.MESH
F32 = jnp.float32
AXES = ("gx", "gy", "gz")
WEIGHT = 0.5


def far_first(n):
    return sorted(range(1, n), key=lambda j: (-min(j, n - j), j))


def rows_loop(lo, count, step, body, carry, unroll):
    whole = count // unroll

    def block(k, c):
        for m in range(unroll):
            c = body(lo + step * (k * unroll + m), c)
        return c

    carry = lax.fori_loop(0, whole, block, carry)
    for m in range(whole * unroll, count):
        carry = body(lo + step * m, carry)
    return carry


def eliminate(excess, coupling, left, e):
    inverse = 1.0 / (excess + coupling + e)
    alpha, beta, leak = e * inverse, coupling * inverse, excess * inverse
    return inverse, alpha, beta, e * leak, e * beta, left + coupling * leak


def ring_factors(nodes):
    n = len(nodes)
    total = [nodes[j][1] + nodes[j - 1][2] for j in range(n)]
    alphas, betas = {}, {}
    coupling, excess, leak1 = nodes[1][0], total[2], total[1]
    for j in range(2, n):
        _, alphas[j], betas[j], carried, coupling, leak1 = eliminate(excess, coupling, leak1, nodes[j][0])
        excess = carried + total[(j + 1) % n]
    leak0 = excess
    c = nodes[0][0] + coupling
    inverse = 1.0 / (leak0 * leak1 + c * (leak0 + leak1))
    to0, to1 = {}, {}
    p, q = jnp.zeros_like(c), jnp.ones_like(c)
    for j in reversed(range(2, n)):
        p, q = betas[j] + alphas[j] * p, alphas[j] * q
        to1[j], to0[j] = p, q
    return [to0[j] for j in range(2, n)] + [to1[j] for j in range(2, n)] + [(leak1 + c) * inverse, c * inverse, (leak0 + c) * inverse]


def ring_apply(factors, loads):
    n = len(loads)
    right = [loads[j][0] + loads[j - 1][1] for j in range(n)]
    sum0, sum1 = right[0], right[1]
    for j in range(2, n):
        sum0 = sum0 + factors(j - 2) * right[j]
        sum1 = sum1 + factors(n - 2 + j - 2) * right[j]
    g00, g01, g11 = (factors(2 * (n - 2) + k) for k in range(3))
    return g00 * sum0 + g01 * sum1, g01 * sum0 + g11 * sum1


def kernel(
    sizes,
    diff_hbm, offset_hbm, v_hbm, c_hbm, dec_hbm, out,
    diff, offset, vx, cx, cy, cz, dec, vy, cyy, vz, czz,
    ax, bx, rx, ay, by, ry, az, bz, rz, segz,
    wx, wy, wz, work1, work2, work3,
    halo_x, halo_y, halo_z,
    mx_own, my_own, mz_own, mx_in, my_in, mz_in,
    fx_own, fy_own, fz_own, fx_in, fy_in, fz_in,
    load_sem, halo_send, halo_recv, mat_send, mat_recv, rhs_send, rhs_recv, known,
):
    me = [lax.axis_index(a) for a in AXES]

    def peer(axis, shift):
        n = sizes[axis]
        return {AXES[axis]: lax.rem(me[axis] + (shift % n), n)}

    def greet(sem, axes):
        for axis in axes:
            for shift in (-1, 1):
                pl.semaphore_signal(sem, inc=1, device_id=peer(axis, shift), device_id_type=MESH)

    def remote(src, dst, send, recv, axis, shift):
        return pltpu.make_async_remote_copy(
            src_ref=src, dst_ref=dst, send_sem=send, recv_sem=recv, device_id=peer(axis, shift), device_id_type=MESH
        )

    barrier = pltpu.get_barrier_semaphore()
    greet(barrier, (0, 1, 2))

    loads = [
        pltpu.make_async_copy(src, dst, load_sem.at[k])
        for k, (src, dst) in enumerate(
            ((v_hbm, vx), (c_hbm.at[2], cz), (diff_hbm, diff), (c_hbm.at[1], cy), (c_hbm.at[0], cx), (dec_hbm, dec), (offset_hbm, offset))
        )
    ]
    for copy in loads:
        copy.start()

    vx2, cy2, cz2, vz2, czz2 = (ref.reshape(1024, 128) for ref in (vx, cy, cz, vz, czz))
    work1_2, work2_2, out2 = (ref.reshape(1024, 128) for ref in (work1, work2, out))

    def into_z(src2, dst2, blocks):
        for b in blocks:
            dst2[pl.ds(b, 128, stride=8), :] = src2[pl.ds(128 * b, 128), :].T

    pl.semaphore_wait(barrier, 6)
    greet(known.at[0], (0, 1, 2))
    halos = [
        remote(v_hbm.at[:, 0, 0, :], halo_y.at[0], halo_send.at[1], halo_recv.at[1], 1, -1),
        remote(v_hbm.at[:, 3, 7, :], halo_y.at[1], halo_send.at[2], halo_recv.at[2], 1, 1),
        remote(c_hbm.at[1, :, 3, 7, :], halo_y.at[2], halo_send.at[3], halo_recv.at[3], 1, 1),
        remote(v_hbm.at[0], halo_x, halo_send.at[0], halo_recv.at[0], 0, -1),
    ]
    for copy in halos:
        copy.start()

    loads[0].wait()
    into_z(vx2, vz2, range(8))
    loads[1].wait()
    into_z(cz2, czz2, range(8))
    halos_z = [
        remote(vz.at[0, 0], halo_z.at[0], halo_send.at[4], halo_recv.at[4], 2, -1),
        remote(vz.at[3, 31], halo_z.at[1], halo_send.at[5], halo_recv.at[5], 2, 1),
        remote(czz.at[3, 31], halo_z.at[2], halo_send.at[6], halo_recv.at[6], 2, 1),
    ]
    for copy in halos_z:
        copy.start()
    pl.semaphore_wait(known.at[0], 6)
    greet(known.at[1], (1, 2))

    for copy in loads[2:]:
        copy.wait()
    scale = [diff[a] * float(c * c) for a, c in enumerate((32, 32, 128))]
    half = [WEIGHT * s for s in scale]

    def to_y(y, _):
        for xc in range(4):
            at = pl.ds(xc * 256 + y, 8, stride=32)
            vy[xc, y] = vx2[at, :]
            cyy[xc, y] = cy2[at, :]
        return 0

    rows_loop(0, 32, 1, to_y, 0, 4)

    def excess_x(i):
        v = vx[i]
        return 1.0 + WEIGHT * (dec[i] * (1.0 + 3.0 * (v * v)))

    def matrix_row(i, carry):
        (kx, lx, sx), (ky, ly, sy), (kz, lz, sz) = carry
        rx[i], ax[i], bx[i], cx_l, kx, sx = eliminate(excess_x(i) + lx, kx, sx, half[0] * cx[i])
        ry[:, i], ay[:, i], by[:, i], cy_l, ky, sy = eliminate(1.0 + ly, ky, sy, half[1] * cyy[:, i])
        rz[:, i], az[:, i], bz[:, i], cz_l, kz, sz = eliminate(1.0 + lz, kz, sz, half[2] * czz[:, i])
        return (kx, cx_l, sx), (ky, cy_l, sy), (kz, cz_l, sz)

    zero = jnp.zeros((4, 8, 128), F32)
    start = (
        (half[0] * cx[0], zero, excess_x(0)),
        (half[1] * cyy[:, 0], zero, zero + 1.0),
        (half[2] * czz[:, 0], zero, zero + 1.0),
    )
    ends = rows_loop(1, 31, 1, matrix_row, start, 1)
    for own, (coupling, carried, left) in zip((mx_own, my_own), ends[:2]):
        own[0], own[1], own[2] = coupling, left, carried
    kz, lz, sz = ends[2]
    coupling, left, excess = kz[0], sz[0], sz[1] + lz[0]
    for s in range(1, 4):
        inverse, alpha, beta, carried, coupling, left = eliminate(excess, coupling, left, kz[s])
        segz[0, s], segz[1, s], segz[2, s] = inverse, alpha, beta
        excess = carried + lz[s] + (sz[s + 1] if s < 3 else 0.0)
    mz_own[0], mz_own[1], mz_own[2] = coupling, left, excess

    def send_matrix(axis, own, into, first, near, far):
        copies = []
        for j in far_first(sizes[axis]):
            if near <= min(j, sizes[axis] - j) <= far:
                k = first + j - 1
                copies.append(remote(own, into.at[j - 1], mat_send.at[k], mat_recv.at[k], axis, -j))
                copies[-1].start()
        return copies

    pl.semaphore_wait(known.at[1], 4)
    greet(known.at[2], (1, 2))
    first_y = sizes[0] - 1
    first_z = first_y + sizes[1] - 1
    mats_x = send_matrix(0, mx_own, mx_in, 0, 1, 2)
    mats_y = send_matrix(1, my_own, my_in, first_y, 1, 3)
    mats_z = send_matrix(2, mz_own, mz_in, first_z, 1, 3)

    halos = halos + halos_z
    for copy in halos:
        copy.wait()

    hy = halo_y.reshape(3, 4, 8, 128)

    def store_y(y, value):
        for xc in range(4):
            work1_2[pl.ds(xc * 256 + y, 8, stride=32), :] = value[xc]

    def flux_y(y, carry):
        v, below = carry
        after = vy[:, y + 1]
        flux = scale[1] * (cyy[:, y] * (after - v))
        store_y(y, flux - below)
        return after, flux

    v0 = vy[:, 0]
    v_last, below = rows_loop(0, 31, 1, flux_y, (v0, scale[1] * (hy[2] * (v0 - hy[1]))), 4)
    store_y(31, scale[1] * (cyy[:, 31] * (hy[0] - v_last)) - below)

    def flux_z(i, carry):
        v, below = carry
        after = vz[:, i + 1]
        flux = scale[2] * (czz[:, i] * (after - v))
        work2[:, i] = flux - below
        return after, flux

    v0 = vz[:, 0]
    c31, v31 = czz[:, 31], vz[:, 31]
    prev_v = jnp.concatenate([halo_z[1][None], v31[:3]], axis=0)
    prev_c = jnp.concatenate([halo_z[2][None], c31[:3]], axis=0)
    next_v = jnp.concatenate([v0[1:], halo_z[0][None]], axis=0)
    v_last, below = rows_loop(0, 31, 1, flux_z, (v0, scale[2] * (prev_c * (v0 - prev_v))), 4)
    work2[:, 31] = scale[2] * (c31 * (next_v - v_last)) - below

    for b in range(8):
        at = pl.ds(128 * b, 128)
        work1_2[at, :] = work1_2[at, :] + work2_2[pl.ds(b, 128, stride=8), :].T

    lane = lax.broadcasted_iota(jnp.int32, (1, 8, 128), 2)
    length = 128 * sizes[2]
    phase = lax.rem(lane + (me[2] * 128 + offset[0]), length).astype(F32) * (2.0 * math.pi / length)
    forcing = 2.0 * jnp.sin(phase)

    def exchange(axis, own, into, first):
        copies = []
        for j in far_first(sizes[axis]):
            k = first + j - 1
            copies.append(remote(own, into.at[j - 1], rhs_send.at[k], rhs_recv.at[k], axis, -j))
            copies[-1].start()
        return copies

    def factors(axis, own, into, weights, copies):
        for copy in copies:
            copy.wait_recv()
        nodes = [tuple(own[k] for k in range(3))] + [tuple(into[j, k] for k in range(3)) for j in range(sizes[axis] - 1)]
        for k, value in enumerate(ring_factors(nodes)):
            weights[k] = value

    def solve(axis, own, into, weight, copies):
        for copy in copies:
            copy.wait_recv()
        pairs = [(own[0], own[1])] + [(into[j, 0], into[j, 1]) for j in range(sizes[axis] - 1)]
        return ring_apply(weight, pairs)

    halves = [slice(2 * c, 2 * c + 2) for c in range(2)]
    sent_x = []
    for c, at in enumerate(halves):

        def right_x(i, v, after, below):
            flux = scale[0] * (cx[i, at] * (after - v))
            right = (flux - below) + work1[i, at] - dec[i, at] * v * (1.0 + v * v) + forcing
            return right, flux

        def forward_x(i, carry):
            v, below, y, load = carry
            after = vx[i + 1, at]
            right, flux = right_x(i, v, after, below)
            y = right + ax[i - 1, at] * y
            work3[i, at] = y
            return after, flux, y, load + bx[i, at] * y

        v0, v1, v2 = vx[0, at], vx[1, at], vx[2, at]
        load, flux = right_x(0, v0, v1, 0.0)
        y, flux = right_x(1, v1, v2, flux)
        work3[1, at] = y
        v, below, y, load = rows_loop(2, 29, 1, forward_x, (v2, flux, y, load + bx[1, at] * y), 2)
        right, flux = right_x(31, v, halo_x[at], below)
        y = right + ax[30, at] * y
        work3[31, at] = y
        fx_own[c, 0] = load + bx[31, at] * y
        fx_own[c, 1] = ax[31, at] * y - flux
        sent_x.append(exchange(0, fx_own.at[c], fx_in.at[c], c * (sizes[0] - 1)))

    pl.semaphore_wait(known.at[2], 4)
    mats_y += send_matrix(1, my_own, my_in, first_y, 4, 4)
    mats_z += send_matrix(2, mz_own, mz_in, first_z, 4, 4)
    factors(0, mx_own, mx_in, wx, mats_x)

    for c, at in enumerate(halves):
        node, after = solve(0, fx_own.at[c], fx_in.at[c], lambda k: wx[k, at], sent_x[c])

        def backward_x(i, u):
            u = (rx[i, at] * work3[i, at] + bx[i, at] * node) + ax[i, at] * u
            work1[i, at] = u
            return u

        rows_loop(31, 31, -1, backward_x, after, 4)
        work1[0, at] = node

    def right_y(y):
        return jnp.stack([work1_2[pl.ds(xc * 256 + y, 8, stride=32), :] for xc in range(4)])

    def forward_y(i, carry):
        y, load = carry
        y = right_y(i) + ay[:, i - 1] * y
        work2[:, i] = y
        return y, load + by[:, i] * y

    y = right_y(1)
    work2[:, 1] = y
    y, load = rows_loop(2, 30, 1, forward_y, (y, right_y(0) + by[:, 1] * y), 3)
    carried = ay[:, 31] * y
    sent_y, first = [], 2 * (sizes[0] - 1)
    for c, at in enumerate(halves):
        fy_own[c, 0] = load[at]
        fy_own[c, 1] = carried[at]
        sent_y.append(exchange(1, fy_own.at[c], fy_in.at[c], first))
        first += sizes[1] - 1

    factors(1, my_own, my_in, wy, mats_y)
    factors(2, mz_own, mz_in, wz, mats_z)

    zwork = work3.reshape(4, 32, 8, 128)
    zwork2 = work3.reshape(1024, 128)
    for c, at in enumerate(halves):
        node, after = solve(1, fy_own.at[c], fy_in.at[c], lambda k: wy[k, at], sent_y[c])

        def store_half(y, value):
            for m in range(2):
                work1_2[pl.ds((2 * c + m) * 256 + y, 8, stride=32), :] = value[m]

        def backward_y(i, u):
            u = (ry[at, i] * work2[at, i] + by[at, i] * node) + ay[at, i] * u
            store_half(i, u)
            return u

        rows_loop(31, 31, -1, backward_y, after, 4)
        store_half(0, node)
        into_z(work1_2, zwork2, range(4 * c, 4 * c + 4))

    def forward_z(i, carry):
        y, load = carry
        y = zwork[:, i] + az[:, i - 1] * y
        work2[:, i] = y
        return y, load + bz[:, i] * y

    y = zwork[:, 1]
    work2[:, 1] = y
    y, load = rows_loop(2, 30, 1, forward_z, (y, zwork[:, 0] + bz[:, 1] * y), 3)
    carried = az[:, 31] * y
    ys, left = [None], load[0]
    for s in range(1, 4):
        y = load[s] + carried[s - 1]
        if s > 1:
            y = y + segz[1, s - 1] * ys[-1]
        ys.append(y)
        left = left + segz[2, s] * y
    fz_own[0] = left
    fz_own[1] = carried[3] + segz[1, 3] * ys[3]

    sent_z = exchange(2, fz_own, fz_in, first)
    node, after = solve(2, fz_own, fz_in, lambda k: wz[k], sent_z)
    ends_z = [after]
    for s in (3, 2, 1):
        ends_z.insert(0, (segz[0, s] * ys[s] + segz[2, s] * node) + segz[1, s] * ends_z[0])
    starts_z = jnp.stack([node] + ends_z[:3])

    def backward_z(i, u):
        u = (rz[:, i] * work2[:, i] + bz[:, i] * starts_z) + az[:, i] * u
        zwork[:, i] = u
        return u

    rows_loop(31, 31, -1, backward_z, jnp.stack(ends_z), 4)
    zwork[:, 0] = starts_z

    for b in range(8):
        at = pl.ds(128 * b, 128)
        out2[at, :] = vx2[at, :] + zwork2[pl.ds(b, 128, stride=8), :].T
    for copy in mats_x + mats_y + mats_z + sum(sent_x, []) + sum(sent_y, []) + sent_z:
        copy.wait_send()


def on_device(sizes, density, conductance, decay_rate, diffusion_numbers, plane_offset):
    nx, ny, nz = sizes
    grid = (32, 4, 8, 128)
    lines = (4, 32, 8, 128)
    one = (4, 8, 128)
    two = (2, 8, 128)
    peers = nx + ny + nz - 3
    vmem = lambda *shape: pltpu.VMEM(shape, F32)
    dma = lambda n: pltpu.SemaphoreType.DMA((n,))
    operands = (
        diffusion_numbers,
        plane_offset,
        density.reshape(grid),
        conductance.reshape((3,) + grid),
        decay_rate.reshape(grid),
    )
    updated = pl.pallas_call(
        functools.partial(kernel, sizes),
        out_shape=jax.ShapeDtypeStruct(grid, F32),
        in_specs=[pl.BlockSpec(memory_space=pl.ANY)] * len(operands),
        out_specs=pl.BlockSpec(memory_space=pltpu.VMEM),
        scratch_shapes=[pltpu.SMEM((3,), F32), pltpu.SMEM((1,), jnp.int32)]
        + [vmem(*grid)] * 5
        + [vmem(*lines)] * 4
        + [vmem(*grid)] * 3
        + [vmem(*lines)] * 6
        + [vmem(3, 4, 8, 128)]
        + [vmem(2 * nx - 1, *one), vmem(2 * ny - 1, *one), vmem(2 * nz - 1, 8, 128)]
        + [vmem(*grid), vmem(*lines), vmem(*grid)]
        + [vmem(*one), vmem(3, 32, 128), vmem(3, 8, 128)]
        + [vmem(3, *one), vmem(3, *one), vmem(3, 8, 128)]
        + [vmem(nx - 1, 3, *one), vmem(ny - 1, 3, *one), vmem(nz - 1, 3, 8, 128)]
        + [vmem(2, 2, *two), vmem(2, 2, *two), vmem(2, 8, 128)]
        + [vmem(2, nx - 1, 2, *two), vmem(2, ny - 1, 2, *two), vmem(nz - 1, 2, 8, 128)]
        + [dma(7), dma(7), dma(7), dma(peers), dma(peers), dma(2 * peers), dma(2 * peers), pltpu.SemaphoreType.REGULAR((3,))],
        compiler_params=pltpu.CompilerParams(collective_id=0, has_side_effects=True, vmem_limit_bytes=40 * 1024 * 1024),
        name="adi_step",
    )(*(x if x.size == 1 else pltpu.with_memory_space_constraint(x, pltpu.MemorySpace.HBM) for x in operands))
    return updated.reshape(density.shape)


def solution(mesh):
    sizes = tuple(mesh.shape[a] for a in AXES)
    placed = (P("gx", "gy", "gz"), P(None, "gx", "gy", "gz"), P("gx", "gy", "gz"), P(), P())
    return jax.shard_map(
        functools.partial(on_device, sizes), mesh=mesh, in_specs=placed, out_specs=P("gx", "gy", "gz"), check_vma=False
    )
```

time: 36.7 us -> 31.2 us (0.85)
  local copies, waits for them, and re-layouts: 4.93 us -> 0.8 us
  Pallas kernels: 30.9 us -> 29.6 us
    unnamed x9 -> x1, local copies, waits for them, and re-layouts: 4.93 us -> 0.8 us
    pallas_call x1, Pallas kernels: 30.9 us -> 29.6 us  [on_device(): pl.pallas_call(functools.partial(kernel, sizes), out_shape=jax.ShapeDtype...]
where the time goes in v1:
time: 31.2 us; the launch traced here: 31.1 us
  Pallas kernels  29.6 us (95%)
  local copies, waits for them, and re-layouts  0.8 us (3%)
  between operations  0.66 us (2%)
    pallas_call x1, Pallas kernels, on_device(): pl.pallas_call(functools.partial(kernel, sizes), out_shape=jax.ShapeDtype...  29.6 us
    unnamed x1, local copies, waits for them, and re-layouts  0.8 us

profile of v1, /device:TPU:1, one launch (start us, length us, event | category | flops | bytes accessed | tf_op | source)
XLA Modules:
  0.0 31.1 jit_solution(385671752204787224)
XLA Ops:
  0.7 29.6 %adi_step.1 = f32[32,4,8,128]{3,2,1,0:T(8,128)S(1)} custom-call(f32[3]{0:T(128)} %diff_hbm.1, s32[1]{0:T(128)S(6)} %copy.7.offset_hbm, f32[32,4,8,128]{3,2,1,0:T(8,128)} %bitcast.6, f32[3,32,4,8,128]{4,3,2,1,0:T(8,128)} %bitcast.5, f32[32,4,8,128]{3,2,1,0:T(8,128)} %bitcast.7), custom_call_target="tpu_custom_call" | custom-call | tf_op jit(solution)/shard_map/adi_step/pallas_call | solution.py:411
  30.3 0.8 %copy.8 = f32[32,32,128]{2,1,0:T(8,128)} copy(f32[32,32,128]{2,1,0:T(8,128)S(1)} %bitcast.4) | data formatting | bytes 1048576

commit v2 on v1

--- a/solution.py
+++ b/solution.py
@@ -19,6 +19,10 @@
 
 
 def rows_loop(lo, count, step, body, carry, unroll):
+    if unroll >= count:
+        for m in range(count):
+            carry = body(lo + step * m, carry)
+        return carry
     whole = count // unroll
 
     def block(k, c):
@@ -71,10 +75,10 @@
 def kernel(
     sizes,
     diff_hbm, offset_hbm, v_hbm, c_hbm, dec_hbm, out,
-    diff, offset, vx, cx, cy, cz, dec, vy, cyy, vz, czz,
+    diff, offset, vx, cx, cy, cz, dec, vy, cyy, czz,
     ax, bx, rx, ay, by, ry, az, bz, rz, segz,
     wx, wy, wz, work1, work2, work3,
-    halo_x, halo_y, halo_z,
+    halo_x, halo_y, halo_z, edge, edge_rows, edge_fix,
     mx_own, my_own, mz_own, mx_in, my_in, mz_in,
     fx_own, fy_own, fz_own, fx_in, fy_in, fz_in,
     load_sem, halo_send, halo_recv, mat_send, mat_recv, rhs_send, rhs_recv, known,
@@ -85,10 +89,12 @@
         n = sizes[axis]
         return {AXES[axis]: lax.rem(me[axis] + (shift % n), n)}
 
-    def greet(sem, axes):
-        for axis in axes:
-            for shift in (-1, 1):
-                pl.semaphore_signal(sem, inc=1, device_id=peer(axis, shift), device_id_type=MESH)
+    near = [(0, -1), (0, 1), (2, -1), (2, 1), (1, -1), (1, 1), (1, -2), (1, 2)]
+    near_z = near[2:4]
+
+    def greet(sem, peers):
+        for axis, shift in peers:
+            pl.semaphore_signal(sem, inc=1, device_id=peer(axis, shift), device_id_type=MESH)
 
     def remote(src, dst, send, recv, axis, shift):
         return pltpu.make_async_remote_copy(
@@ -96,7 +102,7 @@
         )
 
     barrier = pltpu.get_barrier_semaphore()
-    greet(barrier, (0, 1, 2))
+    greet(barrier, near)
 
     loads = [
         pltpu.make_async_copy(src, dst, load_sem.at[k])
@@ -107,16 +113,33 @@
     for copy in loads:
         copy.start()
 
-    vx2, cy2, cz2, vz2, czz2 = (ref.reshape(1024, 128) for ref in (vx, cy, cz, vz, czz))
+    vx2, cy2, cz2, czz2 = (ref.reshape(1024, 128) for ref in (vx, cy, cz, czz))
     work1_2, work2_2, out2 = (ref.reshape(1024, 128) for ref in (work1, work2, out))
 
     def into_z(src2, dst2, blocks):
         for b in blocks:
             dst2[pl.ds(b, 128, stride=8), :] = src2[pl.ds(128 * b, 128), :].T
 
-    pl.semaphore_wait(barrier, 6)
-    greet(known.at[0], (0, 1, 2))
+    lane = lax.broadcasted_iota(jnp.int32, (128, 128), 1)
+    blocks = [pl.ds(128 * b, 128) for b in range(8)]
+    loads[0].wait()
+    packed = jnp.zeros((128, 128), F32)
+    for b, at in enumerate(blocks):
+        packed = jnp.where(lane // 2 == b, pltpu.roll(vx2[at, :], 2 * b + 1, 1), packed)
+    loads[1].wait()
+    for b, at in enumerate(blocks):
+        packed = jnp.where(lane == 16 + b, pltpu.roll(cz2[at, :], 17 + b, 1), packed)
+    edge_rows[...] = packed.T
+    edge[0] = edge_rows[pl.ds(1, 8, stride=2), :]
+    edge[1] = edge_rows[pl.ds(0, 8, stride=2), :]
+    edge[2] = edge_rows[pl.ds(16, 8), :]
+
+    pl.semaphore_wait(barrier, len(near))
+    greet(known.at[0], near)
     halos = [
+        remote(edge.at[0], halo_z.at[0], halo_send.at[4], halo_recv.at[4], 2, -1),
+        remote(edge.at[1], halo_z.at[1], halo_send.at[5], halo_recv.at[5], 2, 1),
+        remote(edge.at[2], halo_z.at[2], halo_send.at[6], halo_recv.at[6], 2, 1),
         remote(v_hbm.at[:, 0, 0, :], halo_y.at[0], halo_send.at[1], halo_recv.at[1], 1, -1),
         remote(v_hbm.at[:, 3, 7, :], halo_y.at[1], halo_send.at[2], halo_recv.at[2], 1, 1),
         remote(c_hbm.at[1, :, 3, 7, :], halo_y.at[2], halo_send.at[3], halo_recv.at[3], 1, 1),
@@ -125,24 +148,13 @@
     for copy in halos:
         copy.start()
 
-    loads[0].wait()
-    into_z(vx2, vz2, range(8))
-    loads[1].wait()
-    into_z(cz2, czz2, range(8))
-    halos_z = [
-        remote(vz.at[0, 0], halo_z.at[0], halo_send.at[4], halo_recv.at[4], 2, -1),
-        remote(vz.at[3, 31], halo_z.at[1], halo_send.at[5], halo_recv.at[5], 2, 1),
-        remote(czz.at[3, 31], halo_z.at[2], halo_send.at[6], halo_recv.at[6], 2, 1),
-    ]
-    for copy in halos_z:
-        copy.start()
-    pl.semaphore_wait(known.at[0], 6)
-    greet(known.at[1], (1, 2))
-
     for copy in loads[2:]:
         copy.wait()
     scale = [diff[a] * float(c * c) for a, c in enumerate((32, 32, 128))]
     half = [WEIGHT * s for s in scale]
+
+    pl.semaphore_wait(known.at[0], len(near))
+    greet(known.at[1], near_z)
 
     def to_y(y, _):
         for xc in range(4):
@@ -151,96 +163,78 @@
             cyy[xc, y] = cy2[at, :]
         return 0
 
-    rows_loop(0, 32, 1, to_y, 0, 4)
+    rows_loop(0, 32, 1, to_y, 0, 32)
 
     def excess_x(i):
         v = vx[i]
         return 1.0 + WEIGHT * (dec[i] * (1.0 + 3.0 * (v * v)))
 
     def matrix_row(i, carry):
-        (kx, lx, sx), (ky, ly, sy), (kz, lz, sz) = carry
+        (kx, lx, sx), (ky, ly, sy) = carry
         rx[i], ax[i], bx[i], cx_l, kx, sx = eliminate(excess_x(i) + lx, kx, sx, half[0] * cx[i])
         ry[:, i], ay[:, i], by[:, i], cy_l, ky, sy = eliminate(1.0 + ly, ky, sy, half[1] * cyy[:, i])
-        rz[:, i], az[:, i], bz[:, i], cz_l, kz, sz = eliminate(1.0 + lz, kz, sz, half[2] * czz[:, i])
-        return (kx, cx_l, sx), (ky, cy_l, sy), (kz, cz_l, sz)
+        return (kx, cx_l, sx), (ky, cy_l, sy)
 
     zero = jnp.zeros((4, 8, 128), F32)
     start = (
         (half[0] * cx[0], zero, excess_x(0)),
         (half[1] * cyy[:, 0], zero, zero + 1.0),
-        (half[2] * czz[:, 0], zero, zero + 1.0),
     )
-    ends = rows_loop(1, 31, 1, matrix_row, start, 1)
-    for own, (coupling, carried, left) in zip((mx_own, my_own), ends[:2]):
+    ends = rows_loop(1, 31, 1, matrix_row, start, 32)
+    for own, (coupling, carried, left) in zip((mx_own, my_own), ends):
         own[0], own[1], own[2] = coupling, left, carried
-    kz, lz, sz = ends[2]
-    coupling, left, excess = kz[0], sz[0], sz[1] + lz[0]
-    for s in range(1, 4):
-        inverse, alpha, beta, carried, coupling, left = eliminate(excess, coupling, left, kz[s])
-        segz[0, s], segz[1, s], segz[2, s] = inverse, alpha, beta
-        excess = carried + lz[s] + (sz[s + 1] if s < 3 else 0.0)
-    mz_own[0], mz_own[1], mz_own[2] = coupling, left, excess
-
-    def send_matrix(axis, own, into, first, near, far):
+    def send_matrix(axis, own, into, first):
         copies = []
         for j in far_first(sizes[axis]):
-            if near <= min(j, sizes[axis] - j) <= far:
-                k = first + j - 1
-                copies.append(remote(own, into.at[j - 1], mat_send.at[k], mat_recv.at[k], axis, -j))
-                copies[-1].start()
+            k = first + j - 1
+            copies.append(remote(own, into.at[j - 1], mat_send.at[k], mat_recv.at[k], axis, -j))
+            copies[-1].start()
         return copies
 
-    pl.semaphore_wait(known.at[1], 4)
-    greet(known.at[2], (1, 2))
     first_y = sizes[0] - 1
     first_z = first_y + sizes[1] - 1
-    mats_x = send_matrix(0, mx_own, mx_in, 0, 1, 2)
-    mats_y = send_matrix(1, my_own, my_in, first_y, 1, 3)
-    mats_z = send_matrix(2, mz_own, mz_in, first_z, 1, 3)
-
-    halos = halos + halos_z
-    for copy in halos:
-        copy.wait()
-
-    hy = halo_y.reshape(3, 4, 8, 128)
-
-    def store_y(y, value):
-        for xc in range(4):
-            work1_2[pl.ds(xc * 256 + y, 8, stride=32), :] = value[xc]
+    mats_x = send_matrix(0, mx_own, mx_in, 0)
+    mats_y = send_matrix(1, my_own, my_in, first_y)
+
+    def at_y(y):
+        return [pl.ds(xc * 256 + y, 8, stride=32) for xc in range(4)]
 
     def flux_y(y, carry):
         v, below = carry
         after = vy[:, y + 1]
         flux = scale[1] * (cyy[:, y] * (after - v))
-        store_y(y, flux - below)
+        for xc, at in enumerate(at_y(y)):
+            work1_2[at, :] = (flux - below)[xc]
         return after, flux
 
-    v0 = vy[:, 0]
-    v_last, below = rows_loop(0, 31, 1, flux_y, (v0, scale[1] * (hy[2] * (v0 - hy[1]))), 4)
-    store_y(31, scale[1] * (cyy[:, 31] * (hy[0] - v_last)) - below)
-
-    def flux_z(i, carry):
-        v, below = carry
-        after = vz[:, i + 1]
-        flux = scale[2] * (czz[:, i] * (after - v))
-        work2[:, i] = flux - below
-        return after, flux
-
-    v0 = vz[:, 0]
-    c31, v31 = czz[:, 31], vz[:, 31]
-    prev_v = jnp.concatenate([halo_z[1][None], v31[:3]], axis=0)
-    prev_c = jnp.concatenate([halo_z[2][None], c31[:3]], axis=0)
-    next_v = jnp.concatenate([v0[1:], halo_z[0][None]], axis=0)
-    v_last, below = rows_loop(0, 31, 1, flux_z, (v0, scale[2] * (prev_c * (v0 - prev_v))), 4)
-    work2[:, 31] = scale[2] * (c31 * (next_v - v_last)) - below
-
-    for b in range(8):
-        at = pl.ds(128 * b, 128)
-        work1_2[at, :] = work1_2[at, :] + work2_2[pl.ds(b, 128, stride=8), :].T
-
-    lane = lax.broadcasted_iota(jnp.int32, (1, 8, 128), 2)
+    v_last, below = rows_loop(0, 31, 1, flux_y, (vy[:, 0], zero), 32)
+    for xc, at in enumerate(at_y(31)):
+        work1_2[at, :] = -below[xc]
+    for at in blocks:
+        v = vx2[at, :]
+        flux = jnp.where(lane < 127, scale[2] * (cz2[at, :] * (pltpu.roll(v, 127, 1) - v)), 0.0)
+        work1_2[at, :] = work1_2[at, :] + (flux - pltpu.roll(flux, 1, 1))
+
+    for copy in halos:
+        copy.wait()
+
+    hy = halo_y.reshape(3, 4, 8, 128)
+    low = scale[1] * (hy[2] * (vy[:, 0] - hy[1]))
+    high = scale[1] * (cyy[:, 31] * (hy[0] - v_last))
+    for xc in range(4):
+        at0, at31 = at_y(0)[xc], at_y(31)[xc]
+        work1_2[at0, :] = work1_2[at0, :] - low[xc]
+        work1_2[at31, :] = work1_2[at31, :] + high[xc]
+    edge_fix[pl.ds(0, 8, stride=2), :] = scale[2] * (edge[2] * (halo_z[0] - edge[1]))
+    edge_fix[pl.ds(1, 8, stride=2), :] = scale[2] * (halo_z[2] * (halo_z[1] - edge[0]))
+    fix = jnp.concatenate([edge_fix[...], jnp.zeros((112, 128), F32)], axis=0).T
+    outer = (lane == 0) | (lane == 127)
+    for b, at in enumerate(blocks):
+        work1_2[at, :] = work1_2[at, :] + jnp.where(outer, pltpu.roll(fix, 127 - 2 * b, 1), 0.0)
+
+    z = lax.broadcasted_iota(jnp.int32, (1, 8, 128), 2)
     length = 128 * sizes[2]
-    phase = lax.rem(lane + (me[2] * 128 + offset[0]), length).astype(F32) * (2.0 * math.pi / length)
+    phase = lax.rem(z + (me[2] * 128 + offset[0]), length).astype(F32) * (2.0 * math.pi / length)
     forcing = 2.0 * jnp.sin(phase)
 
     def exchange(axis, own, into, first):
@@ -285,7 +279,7 @@
         load, flux = right_x(0, v0, v1, 0.0)
         y, flux = right_x(1, v1, v2, flux)
         work3[1, at] = y
-        v, below, y, load = rows_loop(2, 29, 1, forward_x, (v2, flux, y, load + bx[1, at] * y), 2)
+        v, below, y, load = rows_loop(2, 29, 1, forward_x, (v2, flux, y, load + bx[1, at] * y), 32)
         right, flux = right_x(31, v, halo_x[at], below)
         y = right + ax[30, at] * y
         work3[31, at] = y
@@ -293,9 +287,25 @@
         fx_own[c, 1] = ax[31, at] * y - flux
         sent_x.append(exchange(0, fx_own.at[c], fx_in.at[c], c * (sizes[0] - 1)))
 
-    pl.semaphore_wait(known.at[2], 4)
-    mats_y += send_matrix(1, my_own, my_in, first_y, 4, 4)
-    mats_z += send_matrix(2, mz_own, mz_in, first_z, 4, 4)
+    pl.semaphore_wait(known.at[1], len(near_z))
+    greet(known.at[2], near_z)
+    into_z(cz2, czz2, range(8))
+
+    def matrix_row_z(i, carry):
+        kz, lz, sz = carry
+        rz[:, i], az[:, i], bz[:, i], lz, kz, sz = eliminate(1.0 + lz, kz, sz, half[2] * czz[:, i])
+        return kz, lz, sz
+
+    kz, lz, sz = rows_loop(1, 31, 1, matrix_row_z, (half[2] * czz[:, 0], zero, zero + 1.0), 32)
+    coupling, left, excess = kz[0], sz[0], sz[1] + lz[0]
+    for s in range(1, 4):
+        inverse, alpha, beta, carried, coupling, left = eliminate(excess, coupling, left, kz[s])
+        segz[0, s], segz[1, s], segz[2, s] = inverse, alpha, beta
+        excess = carried + lz[s] + (sz[s + 1] if s < 3 else 0.0)
+    mz_own[0], mz_own[1], mz_own[2] = coupling, left, excess
+
+    pl.semaphore_wait(known.at[2], len(near_z))
+    mats_z = send_matrix(2, mz_own, mz_in, first_z)
     factors(0, mx_own, mx_in, wx, mats_x)
 
     for c, at in enumerate(halves):
@@ -306,26 +316,26 @@
             work1[i, at] = u
             return u
 
-        rows_loop(31, 31, -1, backward_x, after, 4)
+        rows_loop(31, 31, -1, backward_x, after, 32)
         work1[0, at] = node
 
-    def right_y(y):
-        return jnp.stack([work1_2[pl.ds(xc * 256 + y, 8, stride=32), :] for xc in range(4)])
-
-    def forward_y(i, carry):
-        y, load = carry
-        y = right_y(i) + ay[:, i - 1] * y
-        work2[:, i] = y
-        return y, load + by[:, i] * y
-
-    y = right_y(1)
-    work2[:, 1] = y
-    y, load = rows_loop(2, 30, 1, forward_y, (y, right_y(0) + by[:, 1] * y), 3)
-    carried = ay[:, 31] * y
     sent_y, first = [], 2 * (sizes[0] - 1)
     for c, at in enumerate(halves):
-        fy_own[c, 0] = load[at]
-        fy_own[c, 1] = carried[at]
+
+        def right_y(y):
+            return jnp.stack([work1_2[pl.ds(xc * 256 + y, 8, stride=32), :] for xc in (2 * c, 2 * c + 1)])
+
+        def forward_y(i, carry):
+            y, load = carry
+            y = right_y(i) + ay[at, i - 1] * y
+            work2[at, i] = y
+            return y, load + by[at, i] * y
+
+        y = right_y(1)
+        work2[at, 1] = y
+        y, load = rows_loop(2, 30, 1, forward_y, (y, right_y(0) + by[at, 1] * y), 32)
+        fy_own[c, 0] = load
+        fy_own[c, 1] = ay[at, 31] * y
         sent_y.append(exchange(1, fy_own.at[c], fy_in.at[c], first))
         first += sizes[1] - 1
 
@@ -346,7 +356,7 @@
             store_half(i, u)
             return u
 
-        rows_loop(31, 31, -1, backward_y, after, 4)
+        rows_loop(31, 31, -1, backward_y, after, 32)
         store_half(0, node)
         into_z(work1_2, zwork2, range(4 * c, 4 * c + 4))
 
@@ -358,7 +368,7 @@
 
     y = zwork[:, 1]
     work2[:, 1] = y
-    y, load = rows_loop(2, 30, 1, forward_z, (y, zwork[:, 0] + bz[:, 1] * y), 3)
+    y, load = rows_loop(2, 30, 1, forward_z, (y, zwork[:, 0] + bz[:, 1] * y), 32)
     carried = az[:, 31] * y
     ys, left = [None], load[0]
     for s in range(1, 4):
@@ -382,7 +392,7 @@
         zwork[:, i] = u
         return u
 
-    rows_loop(31, 31, -1, backward_z, jnp.stack(ends_z), 4)
+    rows_loop(31, 31, -1, backward_z, jnp.stack(ends_z), 32)
     zwork[:, 0] = starts_z
 
     for b in range(8):
@@ -415,13 +425,13 @@
         out_specs=pl.BlockSpec(memory_space=pltpu.VMEM),
         scratch_shapes=[pltpu.SMEM((3,), F32), pltpu.SMEM((1,), jnp.int32)]
         + [vmem(*grid)] * 5
-        + [vmem(*lines)] * 4
+        + [vmem(*lines)] * 3
         + [vmem(*grid)] * 3
         + [vmem(*lines)] * 6
         + [vmem(3, 4, 8, 128)]
         + [vmem(2 * nx - 1, *one), vmem(2 * ny - 1, *one), vmem(2 * nz - 1, 8, 128)]
         + [vmem(*grid), vmem(*lines), vmem(*grid)]
-        + [vmem(*one), vmem(3, 32, 128), vmem(3, 8, 128)]
+        + [vmem(*one), vmem(3, 32, 128), vmem(3, 8, 128), vmem(3, 8, 128), vmem(128, 128), vmem(16, 128)]
         + [vmem(3, *one), vmem(3, *one), vmem(3, 8, 128)]
         + [vmem(nx - 1, 3, *one), vmem(ny - 1, 3, *one), vmem(nz - 1, 3, 8, 128)]
         + [vmem(2, 2, *two), vmem(2, 2, *two), vmem(2, 8, 128)]

time: 31.2 us -> 30.4 us (0.974)
  Pallas kernels: 29.6 us -> 28.8 us
    pallas_call x1, Pallas kernels: 29.6 us -> 28.8 us  [on_device(): pl.pallas_call(functools.partial(kernel, sizes), out_shape=jax.ShapeDtype...]
where the time goes in v2:
time: 30.4 us; the launch traced here: 30.2 us
  Pallas kernels  28.8 us (95%)
  local copies, waits for them, and re-layouts  0.8 us (3%)
  between operations  0.66 us (2%)
    pallas_call x1, Pallas kernels, on_device(): pl.pallas_call(functools.partial(kernel, sizes), out_shape=jax.ShapeDtype...  28.8 us
    unnamed x1, local copies, waits for them, and re-layouts  0.8 us

profile of v2, /device:TPU:1, one launch (start us, length us, event | category | flops | bytes accessed | tf_op | source)
XLA Modules:
  0.0 30.2 jit_solution(3070085766148840620)
XLA Ops:
  0.7 28.8 %adi_step.1 = f32[32,4,8,128]{3,2,1,0:T(8,128)S(1)} custom-call(f32[3]{0:T(128)} %diff_hbm.1, s32[1]{0:T(128)S(6)} %copy.7.offset_hbm, f32[32,4,8,128]{3,2,1,0:T(8,128)} %bitcast.6, f32[3,32,4,8,128]{4,3,2,1,0:T(8,128)} %bitcast.5, f32[32,4,8,128]{3,2,1,0:T(8,128)} %bitcast.7), custom_call_target="tpu_custom_call" | custom-call | tf_op jit(solution)/shard_map/adi_step/pallas_call | solution.py:421
  29.5 0.8 %copy.8 = f32[32,32,128]{2,1,0:T(8,128)} copy(f32[32,32,128]{2,1,0:T(8,128)S(1)} %bitcast.4) | data formatting | bytes 1048576

commit v3 on v2

--- a/solution.py
+++ b/solution.py
@@ -107,7 +107,7 @@
     loads = [
         pltpu.make_async_copy(src, dst, load_sem.at[k])
         for k, (src, dst) in enumerate(
-            ((v_hbm, vx), (c_hbm.at[2], cz), (diff_hbm, diff), (c_hbm.at[1], cy), (c_hbm.at[0], cx), (dec_hbm, dec), (offset_hbm, offset))
+            ((v_hbm, vx), (diff_hbm, diff), (c_hbm.at[0], cx), (dec_hbm, dec), (c_hbm.at[2], cz), (c_hbm.at[1], cy), (offset_hbm, offset))
         )
     ]
     for copy in loads:
@@ -120,13 +120,17 @@
         for b in blocks:
             dst2[pl.ds(b, 128, stride=8), :] = src2[pl.ds(128 * b, 128), :].T
 
+    for copy in loads[:4]:
+        copy.wait()
+    scale = [diff[a] * float(c * c) for a, c in enumerate((32, 32, 128))]
+    half = [WEIGHT * s for s in scale]
+
     lane = lax.broadcasted_iota(jnp.int32, (128, 128), 1)
     blocks = [pl.ds(128 * b, 128) for b in range(8)]
-    loads[0].wait()
     packed = jnp.zeros((128, 128), F32)
     for b, at in enumerate(blocks):
         packed = jnp.where(lane // 2 == b, pltpu.roll(vx2[at, :], 2 * b + 1, 1), packed)
-    loads[1].wait()
+    loads[4].wait()
     for b, at in enumerate(blocks):
         packed = jnp.where(lane == 16 + b, pltpu.roll(cz2[at, :], 17 + b, 1), packed)
     edge_rows[...] = packed.T
@@ -148,13 +152,36 @@
     for copy in halos:
         copy.start()
 
-    for copy in loads[2:]:
-        copy.wait()
-    scale = [diff[a] * float(c * c) for a, c in enumerate((32, 32, 128))]
-    half = [WEIGHT * s for s in scale]
-
+    def excess_x(i):
+        v = vx[i]
+        return 1.0 + WEIGHT * (dec[i] * (1.0 + 3.0 * (v * v)))
+
+    def matrix_row_x(i, carry):
+        kx, lx, sx = carry
+        rx[i], ax[i], bx[i], lx, kx, sx = eliminate(excess_x(i) + lx, kx, sx, half[0] * cx[i])
+        return kx, lx, sx
+
+    zero = jnp.zeros((4, 8, 128), F32)
+    kx, lx, sx = rows_loop(1, 31, 1, matrix_row_x, (half[0] * cx[0], zero, excess_x(0)), 32)
+    mx_own[0], mx_own[1], mx_own[2] = kx, sx, lx
+
+    def send_matrix(axis, own, into, first, reach=(1, 2, 3, 4)):
+        copies = []
+        for j in far_first(sizes[axis]):
+            if min(j, sizes[axis] - j) not in reach:
+                continue
+            k = first + j - 1
+            copies.append(remote(own, into.at[j - 1], mat_send.at[k], mat_recv.at[k], axis, -j))
+            copies[-1].start()
+        return copies
+
+    mats_x = send_matrix(0, mx_own, mx_in, 0, (1,))
     pl.semaphore_wait(known.at[0], len(near))
     greet(known.at[1], near_z)
+    mats_x += send_matrix(0, mx_own, mx_in, 0, (2,))
+
+    for copy in loads[5:]:
+        copy.wait()
 
     def to_y(y, _):
         for xc in range(4):
@@ -165,35 +192,15 @@
 
     rows_loop(0, 32, 1, to_y, 0, 32)
 
-    def excess_x(i):
-        v = vx[i]
-        return 1.0 + WEIGHT * (dec[i] * (1.0 + 3.0 * (v * v)))
-
-    def matrix_row(i, carry):
-        (kx, lx, sx), (ky, ly, sy) = carry
-        rx[i], ax[i], bx[i], cx_l, kx, sx = eliminate(excess_x(i) + lx, kx, sx, half[0] * cx[i])
-        ry[:, i], ay[:, i], by[:, i], cy_l, ky, sy = eliminate(1.0 + ly, ky, sy, half[1] * cyy[:, i])
-        return (kx, cx_l, sx), (ky, cy_l, sy)
-
-    zero = jnp.zeros((4, 8, 128), F32)
-    start = (
-        (half[0] * cx[0], zero, excess_x(0)),
-        (half[1] * cyy[:, 0], zero, zero + 1.0),
-    )
-    ends = rows_loop(1, 31, 1, matrix_row, start, 32)
-    for own, (coupling, carried, left) in zip((mx_own, my_own), ends):
-        own[0], own[1], own[2] = coupling, left, carried
-    def send_matrix(axis, own, into, first):
-        copies = []
-        for j in far_first(sizes[axis]):
-            k = first + j - 1
-            copies.append(remote(own, into.at[j - 1], mat_send.at[k], mat_recv.at[k], axis, -j))
-            copies[-1].start()
-        return copies
-
+    def matrix_row_y(i, carry):
+        ky, ly, sy = carry
+        ry[:, i], ay[:, i], by[:, i], ly, ky, sy = eliminate(1.0 + ly, ky, sy, half[1] * cyy[:, i])
+        return ky, ly, sy
+
+    ky, ly, sy = rows_loop(1, 31, 1, matrix_row_y, (half[1] * cyy[:, 0], zero, zero + 1.0), 32)
+    my_own[0], my_own[1], my_own[2] = ky, sy, ly
     first_y = sizes[0] - 1
     first_z = first_y + sizes[1] - 1
-    mats_x = send_matrix(0, mx_own, mx_in, 0)
     mats_y = send_matrix(1, my_own, my_in, first_y)
 
     def at_y(y):

time: 30.4 us -> 29.2 us (0.961)
  Pallas kernels: 28.8 us -> 27.6 us
    pallas_call x1, Pallas kernels: 28.8 us -> 27.6 us  [on_device(): pl.pallas_call(functools.partial(kernel, sizes), out_shape=jax.ShapeDtype...]
where the time goes in v3:
time: 29.2 us; the launch traced here: 29.1 us
  Pallas kernels  27.6 us (95%)
  local copies, waits for them, and re-layouts  0.8 us (3%)
  between operations  0.66 us (2%)
    pallas_call x1, Pallas kernels, on_device(): pl.pallas_call(functools.partial(kernel, sizes), out_shape=jax.ShapeDtype...  27.6 us
    unnamed x1, local copies, waits for them, and re-layouts  0.8 us

profile of v3, /device:TPU:1, one launch (start us, length us, event | category | flops | bytes accessed | tf_op | source)
XLA Modules:
  0.0 29.1 jit_solution(6013270474091155056)
XLA Ops:
  0.7 27.6 %adi_step.1 = f32[32,4,8,128]{3,2,1,0:T(8,128)S(1)} custom-call(f32[3]{0:T(128)} %diff_hbm.1, s32[1]{0:T(128)S(6)} %copy.7.offset_hbm, f32[32,4,8,128]{3,2,1,0:T(8,128)} %bitcast.6, f32[3,32,4,8,128]{4,3,2,1,0:T(8,128)} %bitcast.5, f32[32,4,8,128]{3,2,1,0:T(8,128)} %bitcast.7), custom_call_target="tpu_custom_call" | custom-call | tf_op jit(solution)/shard_map/adi_step/pallas_call | solution.py:428
  28.3 0.8 %copy.8 = f32[32,32,128]{2,1,0:T(8,128)} copy(f32[32,32,128]{2,1,0:T(8,128)S(1)} %bitcast.4) | data formatting | bytes 1048576

commit v4 on v3

--- a/solution.py
+++ b/solution.py
@@ -141,13 +141,13 @@
     pl.semaphore_wait(barrier, len(near))
     greet(known.at[0], near)
     halos = [
+        remote(vx.at[0], halo_x, halo_send.at[0], halo_recv.at[0], 0, -1),
         remote(edge.at[0], halo_z.at[0], halo_send.at[4], halo_recv.at[4], 2, -1),
         remote(edge.at[1], halo_z.at[1], halo_send.at[5], halo_recv.at[5], 2, 1),
         remote(edge.at[2], halo_z.at[2], halo_send.at[6], halo_recv.at[6], 2, 1),
-        remote(v_hbm.at[:, 0, 0, :], halo_y.at[0], halo_send.at[1], halo_recv.at[1], 1, -1),
-        remote(v_hbm.at[:, 3, 7, :], halo_y.at[1], halo_send.at[2], halo_recv.at[2], 1, 1),
+        remote(vx.at[:, 0, 0, :], halo_y.at[0], halo_send.at[1], halo_recv.at[1], 1, -1),
+        remote(vx.at[:, 3, 7, :], halo_y.at[1], halo_send.at[2], halo_recv.at[2], 1, 1),
         remote(c_hbm.at[1, :, 3, 7, :], halo_y.at[2], halo_send.at[3], halo_recv.at[3], 1, 1),
-        remote(v_hbm.at[0], halo_x, halo_send.at[0], halo_recv.at[0], 0, -1),
     ]
     for copy in halos:
         copy.start()
@@ -165,20 +165,17 @@
     kx, lx, sx = rows_loop(1, 31, 1, matrix_row_x, (half[0] * cx[0], zero, excess_x(0)), 32)
     mx_own[0], mx_own[1], mx_own[2] = kx, sx, lx
 
-    def send_matrix(axis, own, into, first, reach=(1, 2, 3, 4)):
+    def send_matrix(axis, own, into, first):
         copies = []
         for j in far_first(sizes[axis]):
-            if min(j, sizes[axis] - j) not in reach:
-                continue
             k = first + j - 1
             copies.append(remote(own, into.at[j - 1], mat_send.at[k], mat_recv.at[k], axis, -j))
             copies[-1].start()
         return copies
 
-    mats_x = send_matrix(0, mx_own, mx_in, 0, (1,))
     pl.semaphore_wait(known.at[0], len(near))
     greet(known.at[1], near_z)
-    mats_x += send_matrix(0, mx_own, mx_in, 0, (2,))
+    mats_x = send_matrix(0, mx_own, mx_in, 0)
 
     for copy in loads[5:]:
         copy.wait()

time: 29.2 us -> 29 us (level)
  no operation moved by 1% of the time
where the time goes in v4:
time: 29 us; the launch traced here: 28.9 us
  Pallas kernels  27.4 us (94%)
  local copies, waits for them, and re-layouts  0.8 us (3%)
  between operations  0.66 us (2%)
    pallas_call x1, Pallas kernels, on_device(): pl.pallas_call(functools.partial(kernel, sizes), out_shape=jax.ShapeDtype...  27.4 us
    unnamed x1, local copies, waits for them, and re-layouts  0.8 us

profile of v4, /device:TPU:1, one launch (start us, length us, event | category | flops | bytes accessed | tf_op | source)
XLA Modules:
  0.0 28.9 jit_solution(5983306730243331613)
XLA Ops:
  0.7 27.4 %adi_step.1 = f32[32,4,8,128]{3,2,1,0:T(8,128)S(1)} custom-call(f32[3]{0:T(128)} %diff_hbm.1, s32[1]{0:T(128)S(6)} %copy.7.offset_hbm, f32[32,4,8,128]{3,2,1,0:T(8,128)} %bitcast.6, f32[3,32,4,8,128]{4,3,2,1,0:T(8,128)} %bitcast.5, f32[32,4,8,128]{3,2,1,0:T(8,128)} %bitcast.7), custom_call_target="tpu_custom_call" | custom-call | tf_op jit(solution)/shard_map/adi_step/pallas_call | solution.py:425
  28.1 0.8 %copy.8 = f32[32,32,128]{2,1,0:T(8,128)} copy(f32[32,32,128]{2,1,0:T(8,128)S(1)} %bitcast.4) | data formatting | bytes 1048576

commit v5 on v4

--- a/solution.py
+++ b/solution.py
@@ -189,16 +189,8 @@
 
     rows_loop(0, 32, 1, to_y, 0, 32)
 
-    def matrix_row_y(i, carry):
-        ky, ly, sy = carry
-        ry[:, i], ay[:, i], by[:, i], ly, ky, sy = eliminate(1.0 + ly, ky, sy, half[1] * cyy[:, i])
-        return ky, ly, sy
-
-    ky, ly, sy = rows_loop(1, 31, 1, matrix_row_y, (half[1] * cyy[:, 0], zero, zero + 1.0), 32)
-    my_own[0], my_own[1], my_own[2] = ky, sy, ly
     first_y = sizes[0] - 1
     first_z = first_y + sizes[1] - 1
-    mats_y = send_matrix(1, my_own, my_in, first_y)
 
     def at_y(y):
         return [pl.ds(xc * 256 + y, 8, stride=32) for xc in range(4)]
@@ -218,6 +210,15 @@
         v = vx2[at, :]
         flux = jnp.where(lane < 127, scale[2] * (cz2[at, :] * (pltpu.roll(v, 127, 1) - v)), 0.0)
         work1_2[at, :] = work1_2[at, :] + (flux - pltpu.roll(flux, 1, 1))
+
+    def matrix_row_y(i, carry):
+        ky, ly, sy = carry
+        ry[:, i], ay[:, i], by[:, i], ly, ky, sy = eliminate(1.0 + ly, ky, sy, half[1] * cyy[:, i])
+        return ky, ly, sy
+
+    ky, ly, sy = rows_loop(1, 31, 1, matrix_row_y, (half[1] * cyy[:, 0], zero, zero + 1.0), 32)
+    my_own[0], my_own[1], my_own[2] = ky, sy, ly
+    mats_y = send_matrix(1, my_own, my_in, first_y)
 
     for copy in halos:
         copy.wait()

time: 29 us -> 29 us (level)
  no operation moved by 1% of the time
where the time goes in v5:
time: 29 us; the launch traced here: 28.9 us
  Pallas kernels  27.4 us (94%)
  local copies, waits for them, and re-layouts  0.8 us (3%)
  between operations  0.66 us (2%)
    pallas_call x1, Pallas kernels, on_device(): pl.pallas_call(functools.partial(kernel, sizes), out_shape=jax.ShapeDtype...  27.4 us
    unnamed x1, local copies, waits for them, and re-layouts  0.8 us

profile of v5, /device:TPU:1, one launch (start us, length us, event | category | flops | bytes accessed | tf_op | source)
XLA Modules:
  0.0 28.9 jit_solution(3060750691763700134)
XLA Ops:
  0.7 27.4 %adi_step.1 = f32[32,4,8,128]{3,2,1,0:T(8,128)S(1)} custom-call(f32[3]{0:T(128)} %diff_hbm.1, s32[1]{0:T(128)S(6)} %copy.7.offset_hbm, f32[32,4,8,128]{3,2,1,0:T(8,128)} %bitcast.6, f32[3,32,4,8,128]{4,3,2,1,0:T(8,128)} %bitcast.5, f32[32,4,8,128]{3,2,1,0:T(8,128)} %bitcast.7), custom_call_target="tpu_custom_call" | custom-call | tf_op jit(solution)/shard_map/adi_step/pallas_call | solution.py:426
  28.1 0.8 %copy.8 = f32[32,32,128]{2,1,0:T(8,128)} copy(f32[32,32,128]{2,1,0:T(8,128)S(1)} %bitcast.4) | data formatting | bytes 1048576
